TPU v7x, 512 devices: a whole 4x8x8 slice. The times are simulated.
512 devices in a mesh: tgt: 64 (over z, y_hi, core), sup: 8 (over x, y_lo).
Axes of the slice: x: 4, y: 8 (y_hi: 4, y_lo: 2; y = y_hi * 2 + y_lo), z: 8, core: 2. Of those that a mesh axis runs over, the one named last changes fastest.
Arguments:
- targets: float32 [512, 3, 1024], P('tgt'), may hold values from -4 to 4
- labels: int32 [512], P('tgt'), may hold values from 0 to 99
- support_slots: float32 [64, 64, 3, 1024], P('tgt', 'sup'), may hold values from -4 to 4
- block_owner: int32 [4], replicated, may hold values from 0 to 63, as said below
- dual_coeffs: float32 [4, 64, 100], P(None, 'sup'), may hold values from -0.15 to 0.15
Outputs:
- predictions: float32 [512, 100], P('tgt')
- support_grad: float32 [4, 64, 3, 1024], P(None, 'sup')
Inputs may be any that keep to these rules, and one draw needn't show every extreme that they name: 4 distinct slot indices, among them 0 and 63; block b is support_slots[block_owner[b]], and the other slots are never read.
All inputs are finite; a program needn't handle non-finite values.
Results may differ from a plain program's by a relative error of at most 0.0001.
Values sent between devices are 32-bit elements; how exact they have to be, the bound alone decides.
No kernel may reach another device: no remote copies, remote signals or barrier semaphores. Data moves between devices by JAX's collectives and lax.ppermute only.
A program may use at most 64 MiB of HBM per device.

v0:
```python
import jax
import jax.numpy as jnp
from jax import lax
from jax.sharding import PartitionSpec as P

SIDE = 32
LAYERS = 3
weight_variance = 1.6
bias_variance = 0.1
loss_weight = 64.0
arcsin_scale = 2.0 / 3.141592653589793


def broadcast(array, axis, root):
    mine = lax.axis_index(axis) == root
    return lax.psum(jnp.where(mine, array, jnp.zeros_like(array)), axis)


def box_sum(states, grid_side):
    length = states.shape[-1]
    column = lax.broadcasted_iota(jnp.int32, (length,), 0) % grid_side
    zero_column = jnp.zeros(states.shape[:-1] + (1,), states.dtype)
    from_left = jnp.where(
        column > 0, jnp.concatenate([zero_column, states[..., :-1]], axis=-1), 0.0
    )
    from_right = jnp.where(
        column < grid_side - 1, jnp.concatenate([states[..., 1:], zero_column], axis=-1), 0.0
    )
    row_sum = states + from_left + from_right
    zero_row = jnp.zeros(states.shape[:-1] + (grid_side,), states.dtype)
    from_above = jnp.concatenate([zero_row, row_sum[..., :-grid_side]], axis=-1)
    from_below = jnp.concatenate([row_sum[..., grid_side:], zero_row], axis=-1)
    return row_sum + from_above + from_below


def self_chain(images):
    squares = images[:, 0, :] * images[:, 0, :]
    for channel in range(1, images.shape[1]):
        squares = squares + images[:, channel, :] * images[:, channel, :]
    variance = weight_variance * box_sum(squares / images.shape[1], SIDE) / 9.0 + bias_variance
    variances = [variance]
    for layer_index in range(1, LAYERS):
        activated = arcsin_scale * jnp.arcsin(2.0 * variance / (1.0 + 2.0 * variance))
        variance = weight_variance * box_sum(activated, SIDE) / 9.0 + bias_variance
        variances.append(variance)
    return variances


def pair_kernel(support, support_variances, targets, target_variances):
    cross_terms = targets[:, 0, :][:, None, :] * support[:, 0, :][None, :, :]
    for channel in range(1, support.shape[1]):
        cross_terms = (
            cross_terms + targets[:, channel, :][:, None, :] * support[:, channel, :][None, :, :]
        )
    preact = weight_variance * box_sum(cross_terms / support.shape[1], SIDE) / 9.0 + bias_variance
    tangent = preact
    activated = preact
    slope = preact
    for layer_index in range(LAYERS):
        product = (1.0 + 2.0 * target_variances[layer_index])[:, None, :] * (
            1.0 + 2.0 * support_variances[layer_index]
        )[None, :, :]
        activated = arcsin_scale * jnp.arcsin(2.0 * preact / jnp.sqrt(product))
        slope = 2.0 * arcsin_scale / jnp.sqrt(product - 4.0 * preact * preact)
        if layer_index + 1 < LAYERS:
            preact_next = weight_variance * box_sum(activated, SIDE) / 9.0 + bias_variance
            tangent = preact_next + weight_variance * box_sum(tangent * slope, SIDE) / 9.0
            preact = preact_next
    return jnp.mean(weight_variance * (activated + tangent * slope) + bias_variance, axis=-1)


def sum_states(images_part, variance_part):
    return lax.psum((images_part, variance_part), "tgt")


def local(targets, labels, support_slots, block_owner, dual_coeffs):
    own_slot = support_slots[0]
    target_variances = self_chain(targets)
    block_count = dual_coeffs.shape[0]
    classes = dual_coeffs.shape[-1]

    def kernel_rows_of(images, variances):
        return pair_kernel(images, variances, targets, target_variances)

    partial_value = jnp.zeros((targets.shape[0], classes), jnp.float32)
    supports = []
    support_sets = []
    self_pullbacks = []
    pullbacks = []
    for block_index in range(block_count):
        support = broadcast(own_slot, "tgt", block_owner[block_index])
        support_variances, self_pullback = jax.vjp(self_chain, support)
        kernel, pullback = jax.vjp(kernel_rows_of, support, support_variances)
        pullbacks.append(pullback)
        supports.append(support)
        support_sets.append(support_variances)
        self_pullbacks.append(self_pullback)
        partial_value = partial_value + jnp.dot(
            kernel, dual_coeffs[block_index], precision=lax.Precision.HIGHEST
        )
    predictions = lax.psum(partial_value, "sup")
    onehot = (labels[:, None] == lax.broadcasted_iota(jnp.int32, (1, classes), 1)).astype(
        jnp.float32
    )
    residual_error = loss_weight * (predictions - onehot)
    image_terms = []
    variance_terms = []
    for block_index in range(block_count):
        pair_weights = jnp.dot(
            residual_error, dual_coeffs[block_index].T, precision=lax.Precision.HIGHEST
        )
        grad_images, grad_variances = pullbacks[block_index](pair_weights)
        image_terms.append(grad_images)
        variance_terms.append(jnp.stack(grad_variances))
    gradients = []
    for block_index in range(block_count):
        summed_images, summed_variances = sum_states(
            image_terms[block_index], variance_terms[block_index]
        )
        variance_list = [summed_variances[layer_index] for layer_index in range(LAYERS)]
        gradients.append(summed_images + self_pullbacks[block_index](variance_list)[0])
    return (predictions, jnp.stack(gradients))


def solution(mesh):
    return jax.shard_map(
        local,
        mesh=mesh,
        in_specs=(
            P("tgt", None, None),
            P("tgt"),
            P("tgt", "sup", None, None),
            P(),
            P(None, "sup", None),
        ),
        out_specs=(P("tgt", None), P(None, "sup", None, None)),
        check_vma=False,
    )
```

profile of v0, /device:TPU:1, one launch (start us, length us, event | category | flops | bytes accessed | tf_op | source)
XLA Modules:
  0.0 1204.3 jit_solution(16650220429389493855)
XLA Ops:
  7.9 0.7 fusion.412
  11.2 1.6 select_bitcast_fusion.3
  13.0 0.7 copy-done.33
  14.4 545.0 %all-reduce.299.cloned.1.call-done = (f32[8,3,1024]{2,0,1:T(8,128)}, f32[8,3,1024]{2,0,1:T(8,128)}, f32[8,3,1024]{2,0,1:T(8,128)}, f32[8,3,1024]{2,0,1:T(8,128)}) async-done(((f32[8,3,1024]{2,0,1:T(8,128)}, f32[8,3,1024]{2,0,1:T(8,128)}, f32[8,3,1024]{2,0,1:T(8,128)}, f32[8,3,1024]{2,0,1:T(8,128)}), (f32[8,3,1024]{2,0,1:T(8,128)}, f32[8,3,1024]{2,0,1:T(8,128)}, f32[8,3,1024]{2,0,1:T(8,128)}, ...) | async-done | bytes 393232 | tf_op jit(solution)/shard_map/psum | solution.py:16
  559.4 0.9 add_multiply_fusion.34
  560.4 0.9 copy-done.7
  571.4 1.4 fusion.227
  573.2 1.2 add_multiply_fusion.15
  578.1 2.1 add_multiply_fusion.1
  581.3 1.2 add_multiply_fusion.13
  584.9 4.2 add_reduce_fusion
  589.7 15.0 %psum.95 = f32[8,100]{1,0:T(8,128)S(1)} all-reduce(f32[8,100]{1,0:T(8,128)S(1)} %convolution_add_fusion), channel_id=1, replica_groups=mesh['tgt'=64,'sup'=8] {'sup'}, use_global_device_ids=true, to_apply=%region_8.9 | all-reduce | flops 800 | bytes 6400 | tf_op jit(solution)/shard_map/psum | solution.py:101
  604.8 0.9 broadcast_multiply_fusion.13
  605.7 0.9 broadcast_multiply_fusion.12
  606.6 0.9 broadcast_multiply_fusion.11
  607.6 0.9 broadcast_multiply_fusion.14
  608.5 2.8 fusion.206
  612.2 0.8 copy-done.1
  615.0 0.9 slice_select_fusion.15
  615.9 0.9 fusion.205
  616.8 0.9 fusion.211
  617.7 0.9 fusion.155
  620.5 1.0 fusion.204
  621.5 1.0 fusion.146
  622.5 0.9 fusion.125
  626.0 0.9 fusion.207
  626.9 1.0 fusion.116
  634.6 542.6 %all-reduce.297.cloned.1.call-done = (f32[8,3,1024]{2,0,1:T(8,128)}, f32[3,8,1024]{2,1,0:T(8,128)}, f32[8,3,1024]{2,0,1:T(8,128)}, f32[3,8,1024]{2,1,0:T(8,128)}...) async-done(((f32[8,3,1024]{2,0,1:T(8,128)}, f32[3,8,1024]{2,1,0:T(8,128)}, f32[8,3,1024]{2,0,1:T(8,128)}, ...) | async-done | bytes 786448 | tf_op jit(solution)/shard_map/psum | solution.py:73
  1177.3 0.8 fusion.240
  1178.1 0.8 fusion.247
  1179.4 0.7 copy-done.40
  1180.3 0.7 copy-done.46
  1181.1 0.8 copy-done.50
  1183.3 0.7 copy-done.28
  1184.1 0.7 copy-done.32
  1185.0 0.7 copy-done.30
  1185.8 0.8 copy-done.47
  1187.1 0.8 copy-done.10
  1188.0 0.9 copy-done.8
  1188.9 0.9 copy-done.6
  1189.9 0.7 copy-done.42
  1191.0 0.7 copy-done.26
  1192.0 0.8 copy-done.4
  1192.9 0.9 copy-done.57
  1193.8 0.9 copy-done.56
  1194.7 0.9 copy-done.55
  1195.6 0.9 copy-done.54
  1196.5 0.8 pad_maximum_fusion
  (339 shorter events, 37.3 us)
Async XLA Ops:
  7.2 552.2 %all-reduce.299.cloned.1.call-start = ((), (), s32[]{:S(2)}) async-start(), calls=%async_computation.1 | async-start | bytes 786432 | tf_op jit(solution)/shard_map/psum | solution.py:16
  12.8 0.9 copy-start.33
  12.8 1164.4 %all-reduce.297.cloned.1.call-start = ((), (), s32[]{:S(2)}) async-start(), calls=%async_computation | async-start | bytes 1572864 | tf_op jit(solution)/shard_map/psum | solution.py:73
  559.4 1.0 copy-start.3
  559.4 1.0 copy-start.5
  560.4 0.9 copy-start.7
  560.4 0.9 copy-start.9
  562.0 11.2 copy-start.17
  563.7 17.7 %copy-start.21 = (f32[8,1024]{1,0:T(8,128)}, f32[8,1024]{1,0:T(8,128)S(1)}, u32[]{:S(2)}) copy-start(f32[8,1024]{1,0:T(8,128)S(1)} %get-tuple-element.409) | copy-start | bytes 98308
  564.3 9.0 copy-start.15
  565.2 0.8 copy-start.39
  566.7 14.6 %copy-start.19 = (f32[8,1024]{1,0:T(8,128)}, f32[8,1024]{1,0:T(8,128)S(1)}, u32[]{:S(2)}) copy-start(f32[8,1024]{1,0:T(8,128)S(1)} %get-tuple-element.407) | copy-start | bytes 98308
  567.8 10.3 copy-start.13
  568.9 9.2 copy-start.11
  584.4 4.7 copy-start.37
  584.9 4.2 copy-start.58
  604.8 2.8 copy-start.60
  604.8 3.7 copy-start
  612.0 1.0 copy-start.1
  612.0 1.0 copy-start.2
  612.0 1.0 copy-start.24
  612.0 1.0 copy-start.38
  614.9 0.9 copy-start.20
  615.0 0.9 copy-start.22
  615.9 0.9 copy-start.12
  615.9 0.9 copy-start.14
  619.8 0.8 copy-start.18
  625.2 0.8 copy-start.16
  630.8 0.8 copy-start.52
  630.8 0.8 copy-start.53
  1177.3 1.6 copy-start.48
  1177.3 1.6 copy-start.49
  1179.3 0.8 copy-start.40
  1180.2 0.8 copy-start.46
  1181.0 0.9 copy-start.50
  1182.2 0.8 copy-start.44
  1183.2 0.8 copy-start.28
  1184.0 0.8 copy-start.32
  1185.7 0.9 copy-start.47
  1187.0 0.9 copy-start.10
  1187.9 0.9 copy-start.8
  1188.9 0.9 copy-start.6
  1190.9 0.8 copy-start.26
  1191.9 0.9 copy-start.4
  1192.9 0.9 copy-start.57
  1193.8 0.9 copy-start.56
  1194.7 0.9 copy-start.55
  1195.6 0.9 copy-start.54
  (15 other events, 9.6 us)
Sparse Core Ops, SparseCore 0:
  12.9 546.3 all-reduce.298
  634.8 542.4 all-reduce.296
where the time goes:
time: 1210 us; the launch traced here: 1200 us
  waiting for transfers between devices  1090 us (90%)
  other arithmetic  46 us (4%)
  local copies, waits for them, and re-layouts  33.1 us (3%)
  between operations  18.3 us (2%)
  blocking collectives  15 us (1%)
    psum x1, waiting for transfers between devices, broadcast(): return lax.psum(jnp.where(mine, array, jnp.zeros_like(array)), axis)  545 us
    psum x1, waiting for transfers between devices, sum_states(): return lax.psum((images_part, variance_part), 'tgt')  543 us
  transfers between devices with their start and end apart: 2, of which 2 were waited for; matrix products, arithmetic and copies ran while one was open for 0% of the time, Pallas kernels for 0%

commit v1 on v0

--- a/solution.py
+++ b/solution.py
@@ -13,7 +13,7 @@
 
 def broadcast(array, axis, root):
     mine = lax.axis_index(axis) == root
-    return lax.psum(jnp.where(mine, array, jnp.zeros_like(array)), axis)
+    return jnp.sum(lax.all_gather(jnp.where(mine, array, jnp.zeros_like(array)), axis), axis=0)
 
 
 def box_sum(states, grid_side):

time: 1210 us -> 1040 us (0.86)
  waiting for transfers between devices: 1090 us -> 910 us
  other arithmetic: 46 us -> 67.5 us
  local copies, waits for them, and re-layouts: 33.1 us -> 14.3 us
    psum x1 -> x0, waiting for transfers between devices: 545 us -> none  [broadcast(): return lax.psum(jnp.where(mine, array, jnp.zeros_like(array)), axis)]
    all_gather x0 -> x4, waiting for transfers between devices: none -> 368 us  [broadcast(): lax.all_gather(jnp.where(mine, array, jnp.zeros_like(array)), axis)]
    unnamed x122 -> x110, local copies, waits for them, and re-layouts: 21 us -> 0.23 us
    reduce_sum x0 -> x4, other arithmetic: none -> 12.5 us  [broadcast(): jnp.sum(lax.all_gather(jnp.where(mine, array, jnp.zeros_like(array)), axi...]
  transfers between devices with their start and end apart: 2 -> 5, of which waited for: 2 -> 5; matrix products, arithmetic and copies ran while one was open for 0% -> 1% of each run, Pallas kernels for 0% -> 0%
where the time goes in v1:
time: 1040 us; the launch traced here: 1030 us
  waiting for transfers between devices  910 us (88%)
  other arithmetic  67.5 us (6%)
  between operations  18.3 us (2%)
  blocking collectives  14.4 us (1%)
  local copies, waits for them, and re-layouts  14.3 us (1%)
    psum x1, waiting for transfers between devices, sum_states(): return lax.psum((images_part, variance_part), 'tgt')  541 us
    all_gather x4, waiting for transfers between devices, broadcast(): lax.all_gather(jnp.where(mine, array, jnp.zeros_like(array)), axis)  368 us
  transfers between devices with their start and end apart: 5, of which 5 were waited for; matrix products, arithmetic and copies ran while one was open for 1% of the time, Pallas kernels for 0%

profile of v1, /device:TPU:1, one launch (start us, length us, event | category | flops | bytes accessed | tf_op | source)
XLA Modules:
  0.0 1029.4 jit_solution(7396323300032595711)
XLA Ops:
  7.2 1.4 fusion.412
  11.2 1.6 broadcast_select_fusion.3
  15.0 1.4 broadcast_multiply_fusion.5
  16.5 0.8 slice_bitcast_fusion.22
  17.3 96.4 %all-gather.7.cloned.1.call-done = f32[64,8,3,1024]{3,1,2,0:T(8,128)} async-done(((f32[1,8,3,1024]{3,1,2,0:T(8,128)}), f32[64,8,3,1024]{3,1,2,0:T(8,128)}) %all-gather.7.cloned.1.call-update) | async-done | bytes 6291472 | tf_op jit(solution)/shard_map/all_gather | solution.py:16
  113.7 3.1 reduce_sum.282
  116.9 90.3 %all-gather.11.cloned.1.call-done = f32[64,8,3,1024]{3,1,2,0:T(8,128)} async-done(((f32[1,8,3,1024]{3,1,2,0:T(8,128)}), f32[64,8,3,1024]{3,1,2,0:T(8,128)}) %all-gather.11.cloned.1.call-update) | async-done | bytes 6291472 | tf_op jit(solution)/shard_map/all_gather | solution.py:16
  207.2 3.1 reduce_sum.289
  210.3 90.3 %all-gather.9.cloned.1.call-done = f32[64,8,3,1024]{3,1,2,0:T(8,128)} async-done(((f32[1,8,3,1024]{3,1,2,0:T(8,128)}), f32[64,8,3,1024]{3,1,2,0:T(8,128)}) %all-gather.9.cloned.1.call-update) | async-done | bytes 6291472 | tf_op jit(solution)/shard_map/all_gather | solution.py:16
  300.6 3.1 reduce_sum.287
  303.9 90.6 %all-gather.5.cloned.1.call-done = f32[64,8,3,1024]{3,1,2,0:T(8,128)} async-done(((f32[1,8,3,1024]{3,1,2,0:T(8,128)}), f32[64,8,3,1024]{3,1,2,0:T(8,128)}) %all-gather.5.cloned.1.call-update) | async-done | bytes 6291472 | tf_op jit(solution)/shard_map/all_gather | solution.py:16
  394.5 3.1 reduce_sum.280
  405.3 1.4 fusion.227
  407.1 1.2 add_multiply_fusion.15
  412.5 1.7 add_multiply_fusion.1
  415.3 1.2 add_multiply_fusion.13
  418.3 4.4 add_reduce_fusion
  423.2 14.4 %psum.63 = f32[8,100]{1,0:T(8,128)S(1)} all-reduce(f32[8,100]{1,0:T(8,128)S(1)} %convolution_add_fusion), channel_id=1, replica_groups=mesh['tgt'=64,'sup'=8] {'sup'}, use_global_device_ids=true, to_apply=%region_8.9 | all-reduce | flops 800 | bytes 6400 | tf_op jit(solution)/shard_map/psum | solution.py:101
  437.7 1.0 broadcast_multiply_fusion.13
  438.7 0.9 broadcast_multiply_fusion.12
  439.6 0.9 broadcast_multiply_fusion.11
  440.5 0.9 broadcast_multiply_fusion.14
  441.4 3.0 fusion.206
  447.2 0.9 slice_select_fusion.15
  448.2 0.9 fusion.205
  449.1 0.9 fusion.211
  450.0 0.9 fusion.155
  452.5 0.9 fusion.204
  453.5 1.0 fusion.146
  454.4 0.9 fusion.125
  457.9 0.9 fusion.207
  458.8 1.0 fusion.116
  466.4 540.9 %all-reduce.295.cloned.1.call-done = (f32[8,3,1024]{2,0,1:T(8,128)}, f32[3,8,1024]{2,1,0:T(8,128)}, f32[8,3,1024]{2,0,1:T(8,128)}, f32[3,8,1024]{2,1,0:T(8,128)}...) async-done(((f32[8,3,1024]{2,0,1:T(8,128)}, f32[3,8,1024]{2,1,0:T(8,128)}, f32[8,3,1024]{2,0,1:T(8,128)}, ...) | async-done | bytes 786448 | tf_op jit(solution)/shard_map/psum | solution.py:73
  1007.3 0.8 fusion.240
  1008.2 0.8 fusion.247
  1008.9 0.8 fusion.254
  1009.7 0.8 fusion.261
  1010.8 0.8 pad_add_fusion.47
  1011.6 0.8 pad_add_fusion.44
  1012.5 0.8 fusion.257
  1013.5 0.9 fusion.264
  1014.4 0.8 pad_add_fusion.41
  1015.5 0.8 fusion.250
  1016.6 0.9 fusion.253
  1017.5 0.9 fusion.267
  1018.5 0.9 fusion.260
  1019.4 0.8 pad_add_fusion.38
  1021.8 0.8 pad_maximum_fusion
  (342 shorter events, 33.1 us)
Async XLA Ops:
  7.2 106.6 %all-gather.7.cloned.1.call-start = ((), (), s32[]{:S(2)}) async-start(), calls=%async_computation.1 | async-start | bytes 6389760 | tf_op jit(solution)/shard_map/all_gather | solution.py:16
  12.8 194.3 %all-gather.11.cloned.1.call-start = ((), (), s32[]{:S(2)}) async-start(), calls=%async_computation.3 | async-start | bytes 6389760 | tf_op jit(solution)/shard_map/all_gather | solution.py:16
  13.6 287.0 %all-gather.9.cloned.1.call-start = ((), (), s32[]{:S(2)}) async-start(), calls=%async_computation.2 | async-start | bytes 6389760 | tf_op jit(solution)/shard_map/all_gather | solution.py:16
  14.3 380.2 %all-gather.5.cloned.1.call-start = ((), (), s32[]{:S(2)}) async-start(), calls=%async_computation | async-start | bytes 6389760 | tf_op jit(solution)/shard_map/all_gather | solution.py:16
  14.9 992.4 %all-reduce.295.cloned.1.call-start = ((), (), s32[]{:S(2)}) async-start(), calls=%async_computation.4 | async-start | bytes 1572864 | tf_op jit(solution)/shard_map/psum | solution.py:73
  398.2 5.3 copy-start.30
  398.2 8.9 copy-start.18
  399.1 8.0 copy-start
  399.4 15.8 %copy-start.14 = (f32[8,1024]{1,0:T(8,128)}, f32[8,1024]{1,0:T(8,128)S(1)}, u32[]{:S(2)}) copy-start(f32[8,1024]{1,0:T(8,128)S(1)} %get-tuple-element.405) | copy-start | bytes 98308
  399.7 15.5 %copy-start.2 = (f32[8,1024]{1,0:T(8,128)}, f32[8,1024]{1,0:T(8,128)S(1)}, u32[]{:S(2)}) copy-start(f32[8,1024]{1,0:T(8,128)S(1)} %get-tuple-element.316) | copy-start | bytes 98308
  400.0 7.1 copy-start.16
  400.6 1.9 copy-start.41
  400.8 3.3 copy-start.26
  400.8 4.5 copy-start.8
  401.2 3.2 copy-start.24
  401.2 4.1 copy-start.6
  401.6 13.6 %copy-start.20 = (f32[8,1024]{1,0:T(8,128)}, f32[8,1024]{1,0:T(8,128)S(1)}, u32[]{:S(2)}) copy-start(f32[8,1024]{1,0:T(8,128)S(1)} %get-tuple-element.403) | copy-start | bytes 98308
  402.1 2.4 copy-start.43
  402.4 2.2 copy-start.39
  402.7 9.8 copy-start.10
  402.7 9.8 copy-start.12
  417.4 5.3 copy-start.53
  418.0 4.7 copy-start.32
  418.1 4.8 copy-start.33
  418.1 4.8 copy-start.35
  418.3 4.4 copy-start.22
  418.3 4.6 copy-start.34
  437.7 8.4 copy-start.54
  437.7 7.5 copy-start.4
  437.7 7.5 copy-start.5
  437.7 7.5 copy-start.23
  437.7 7.5 copy-start.36
  458.8 4.6 copy-start.46
  458.8 4.6 copy-start.47
  458.8 4.6 copy-start.48
  460.1 552.4 %copy-start.42 = (f32[8,1024]{1,0:T(8,128)S(1)}, f32[8,1024]{1,0:T(8,128)}, u32[]{:S(2)}) copy-start(f32[8,1024]{1,0:T(8,128)} %copy-done.41) | copy-start | bytes 98308
  460.1 553.4 %copy-start.38 = (f32[8,1024]{1,0:T(8,128)S(1)}, f32[8,1024]{1,0:T(8,128)}, u32[]{:S(2)}) copy-start(f32[8,1024]{1,0:T(8,128)} %copy-done.37) | copy-start | bytes 98308
  460.3 555.2 %copy-start.44 = (f32[8,1024]{1,0:T(8,128)S(1)}, f32[8,1024]{1,0:T(8,128)}, u32[]{:S(2)}) copy-start(f32[8,1024]{1,0:T(8,128)} %copy-done.43) | copy-start | bytes 98308
  460.4 556.2 %copy-start.27 = (f32[8,1024]{1,0:T(8,128)S(1)}, f32[8,1024]{1,0:T(8,128)}, u32[]{:S(2)}) copy-start(f32[8,1024]{1,0:T(8,128)} %copy-done.26) | copy-start | bytes 98308
  460.4 557.1 %copy-start.31 = (f32[8,1024]{1,0:T(8,128)S(1)}, f32[8,1024]{1,0:T(8,128)}, u32[]{:S(2)}) copy-start(f32[8,1024]{1,0:T(8,128)} %copy-done.30) | copy-start | bytes 98308
  460.6 557.9 %copy-start.29 = (f32[8,1024]{1,0:T(8,128)S(1)}, f32[8,1024]{1,0:T(8,128)}, u32[]{:S(2)}) copy-start(f32[8,1024]{1,0:T(8,128)} %copy-done.28) | copy-start | bytes 98308
  460.8 560.1 %copy-start.40 = (f32[8,1024]{1,0:T(8,128)S(1)}, f32[8,1024]{1,0:T(8,128)}, u32[]{:S(2)}) copy-start(f32[8,1024]{1,0:T(8,128)} %copy-done.39) | copy-start | bytes 98308
  462.7 558.5 %copy-start.25 = (f32[8,1024]{1,0:T(8,128)S(1)}, f32[8,1024]{1,0:T(8,128)}, u32[]{:S(2)}) copy-start(f32[8,1024]{1,0:T(8,128)} %copy-done.24) | copy-start | bytes 98308
  1007.3 13.6 %copy-start.45 = (f32[3,8,1024]{2,1,0:T(8,128)S(1)}, f32[3,8,1024]{2,1,0:T(8,128)}, u32[]{:S(2)}) copy-start(f32[3,8,1024]{2,1,0:T(8,128)} %get-tuple-element.39) | copy-start | bytes 294916
  1007.3 14.4 %copy-start.52 = (f32[8,3,1024]{2,0,1:T(8,128)S(1)}, f32[8,3,1024]{2,0,1:T(8,128)}, u32[]{:S(2)}) copy-start(f32[8,3,1024]{2,0,1:T(8,128)} %get-tuple-element.44) | copy-start | bytes 294916
  1007.3 14.4 %copy-start.51 = (f32[8,3,1024]{2,0,1:T(8,128)S(1)}, f32[8,3,1024]{2,0,1:T(8,128)}, u32[]{:S(2)}) copy-start(f32[8,3,1024]{2,0,1:T(8,128)} %get-tuple-element.42) | copy-start | bytes 294916
  1007.3 14.4 %copy-start.50 = (f32[8,3,1024]{2,0,1:T(8,128)S(1)}, f32[8,3,1024]{2,0,1:T(8,128)}, u32[]{:S(2)}) copy-start(f32[8,3,1024]{2,0,1:T(8,128)} %get-tuple-element.40) | copy-start | bytes 294916
  1007.3 14.5 %copy-start.49 = (f32[8,3,1024]{2,0,1:T(8,128)S(1)}, f32[8,3,1024]{2,0,1:T(8,128)}, u32[]{:S(2)}) copy-start(f32[8,3,1024]{2,0,1:T(8,128)} %get-tuple-element.38) | copy-start | bytes 294916
  (12 other events, 18.4 us)
Sparse Core Ops, SparseCore 0:
  13.0 100.7 all-gather.6
  117.1 90.0 all-gather.10
  210.5 90.0 all-gather.8
  304.4 90.0 all-gather.4
  466.5 540.7 all-reduce.294
